TPU v7x, 32 devices: a whole 2x2x4 slice. The times are simulated.
32 devices in a mesh: grp: 2 (over core), mr: 8 (over z, y), mc: 2 (over x).
Axes of the slice: x: 2, y: 2, z: 4, core: 2. Of those that a mesh axis runs over, the one named last changes fastest.
Arguments:
- queries: bfloat16 [384, 8192], P(('grp', 'mr'), 'mc'), may hold values from -6 to 6
- new_keys: bfloat16 [384, 1024], P(('grp', 'mr'), 'mc'), may hold values from -6 to 6
- new_values: bfloat16 [384, 1024], P(('grp', 'mr'), 'mc'), may hold values from -6 to 6
- key_cache: bfloat16 [384, 512, 1024], P(('grp', 'mr'), None, 'mc'), may hold values from -6 to 6
- value_cache: bfloat16 [384, 512, 1024], P(('grp', 'mr'), None, 'mc'), may hold values from -6 to 6
- context_len: int32 [384], P(('grp', 'mr')), may hold values from 2 to 512, as said below
- cache_slot: int32 [384], P(('grp', 'mr')), may hold values from 0 to 383, as said below
- residual_in: bfloat16 [384, 8192], P(('grp', 'mr'), 'mc'), may hold values from -31 to 31
- out_weight: bfloat16 [8192, 8192], P(('grp', 'mr'), 'mc'), may hold values from -0.25 to 0.25
- gate_weight: bfloat16 [8192, 28672], P('mc', ('grp', 'mr')), may hold values from -0.0625 to 0.0625
- up_weight: bfloat16 [8192, 28672], P('mc', ('grp', 'mr')), may hold values from -0.0625 to 0.0625
Outputs:
- residual_out: bfloat16 [384, 8192], P(('grp', 'mr'), 'mc')
- activation: bfloat16 [384, 28672], P('mc', ('grp', 'mr'))
Inputs may be any that keep to these rules, and one draw needn't show every extreme that they name: Row r's history fills positions 0 to context_len[r] - 1 of its cache row; some row has 512. `cache_slot`: within each aligned block of 24 rows the values are a permutation of that block's own row indices.
All inputs are finite; a program needn't handle non-finite values.
Results may differ from a plain program's by a relative error of at most 0.006.
Values may be sent and summed in bfloat16 or wider, within the bound.
A program may use at most 128 MiB of HBM per device.

v0:
```python
import jax
import jax.numpy as jnp
from jax import lax
from jax.sharding import PartitionSpec as P

D = 8192
HD = 128
norm_epsilon = 1e-05
masked_score = -1e30


def attend_rows(queries, new_keys, new_values, key_rows, value_rows, context_len):
    row_denominator_sum = queries.shape[0]
    context = key_rows.shape[1]
    kv_heads = key_rows.shape[2] // HD
    groups = queries.shape[1] // key_rows.shape[2]
    attention_logit_scale = HD ** (-0.5)
    query_grouped_four = queries.reshape(row_denominator_sum, kv_heads, groups, HD)
    key_four = key_rows.reshape(row_denominator_sum, context, kv_heads, HD)
    value_four = value_rows.reshape(row_denominator_sum, context, kv_heads, HD)
    current_key = new_keys.reshape(row_denominator_sum, kv_heads, HD)
    own_value = new_values.reshape(row_denominator_sum, kv_heads, HD).astype(jnp.float32)
    scores = (
        jnp.einsum(
            "bkgd,bckd->bkgc", query_grouped_four, key_four, preferred_element_type=jnp.float32
        )
        * attention_logit_scale
    )
    positions = jnp.arange(context, dtype=jnp.int32)
    valid_mask = positions[None, :] < context_len[:, None]
    scores = jnp.where(valid_mask[:, None, None, :], scores, masked_score)
    current_score = (
        jnp.einsum(
            "cnhz,cnz->cnh", query_grouped_four, current_key, preferred_element_type=jnp.float32
        )
        * attention_logit_scale
    )
    row_max = jnp.maximum(jnp.max(scores, axis=3), current_score)
    exponent = jnp.exp(scores - row_max[..., None])
    own_exponent = jnp.exp(current_score - row_max)
    denominator = jnp.sum(exponent, axis=3) + own_exponent
    weights = (exponent / denominator[..., None]).astype(jnp.bfloat16)
    own_weight = (own_exponent / denominator).astype(jnp.bfloat16).astype(jnp.float32)
    combined = jnp.einsum(
        "bkgc,bckd->bkgd", weights, value_four, preferred_element_type=jnp.float32
    )
    combined = combined + own_weight[..., None] * own_value[:, :, None, :]
    return combined.reshape(row_denominator_sum, -1).astype(jnp.bfloat16)


def body(
    queries,
    new_keys,
    new_values,
    key_cache,
    value_cache,
    context_len,
    cache_slot,
    residual_in,
    out_weight,
    gate_weight,
    up_weight,
):
    local_rows = queries.shape[0]
    row_base = lax.axis_index(("grp", "mr")) * local_rows
    device_slot_index = cache_slot - row_base
    positions = jnp.arange(local_rows, dtype=jnp.int32)
    matches = device_slot_index[:, None] == positions[None, :]
    inverse = jnp.sum(jnp.where(matches, positions[:, None], 0), axis=0)
    by_cache = attend_rows(
        jnp.take(queries, inverse, axis=0),
        jnp.take(new_keys, inverse, axis=0),
        jnp.take(new_values, inverse, axis=0),
        key_cache,
        value_cache,
        jnp.take(context_len, inverse, axis=0),
    )
    attended = jnp.take(by_cache, device_slot_index, axis=0)
    gathered = lax.all_gather(attended, "mc", axis=1, tiled=True)
    features = lax.all_to_all(gathered, ("grp", "mr"), split_axis=1, concat_axis=0, tiled=True)
    groups = lax.axis_size("grp")
    rows = features.shape[0]
    group_rows = rows // groups
    group = lax.axis_index("grp")
    own_share = None
    for shift in range(groups - 1, -1, -1):
        target = lax.rem(group + shift, groups)
        block = lax.dynamic_slice_in_dim(features, target * group_rows, group_rows, axis=0)
        term = jnp.dot(block, out_weight, preferred_element_type=jnp.float32)
        if shift > 0:
            pairs = [(i, (i + shift) % groups) for i in range(groups)]
            term = lax.ppermute(term.astype(jnp.bfloat16), "grp", pairs).astype(jnp.float32)
        own_share = term if own_share is None else own_share + term
    shares = lax.psum_scatter(
        own_share.astype(jnp.bfloat16), "mr", scatter_dimension=0, tiled=True
    ).astype(jnp.float32)
    residual_out = (residual_in.astype(jnp.float32) + shares).astype(jnp.bfloat16)
    group_part = lax.all_gather(residual_out, "mr", axis=0, tiled=True)
    everyone = lax.all_gather(group_part, "grp", axis=0, tiled=True) if groups != 2 else None
    if groups == 2:
        other_part = lax.ppermute(group_part, "grp", [(0, 1), (1, 0)])
        first = jnp.where(group == 0, group_part, other_part)
        second = jnp.where(group == 0, other_part, group_part)
        everyone = jnp.concatenate([first, second], axis=0)
    widened = lax.optimization_barrier(everyone).astype(jnp.float32)
    squares = jnp.sum(widened * widened, axis=1)
    square_sum = scatter_sum(squares, jnp.float32)
    gate_term = jnp.dot(everyone, gate_weight, preferred_element_type=jnp.float32)
    gate_sum = scatter_sum(gate_term, jnp.bfloat16)
    up_term = jnp.dot(everyone, up_weight, preferred_element_type=jnp.float32)
    up_sum = scatter_sum(up_term, jnp.bfloat16)
    inverse_rms = lax.rsqrt(square_sum / D + norm_epsilon)
    gate_value = gate_sum * inverse_rms[:, None]
    upward = up_sum * inverse_rms[:, None]
    activation = (jax.nn.silu(gate_value) * upward).astype(jnp.bfloat16)
    return (residual_out, activation)


def scatter_sum(term, kind):
    count = lax.axis_size("mc")
    me = lax.axis_index("mc")
    kept = term.shape[0] // count
    total = lax.dynamic_slice_in_dim(term, me * kept, kept, axis=0)
    for shift in range(1, count):
        target = lax.rem(me + shift, count)
        sent = lax.dynamic_slice_in_dim(term, target * kept, kept, axis=0).astype(kind)
        pairs = [(i, (i + shift) % count) for i in range(count)]
        total = total + lax.ppermute(sent, "mc", pairs).astype(jnp.float32)
    return total


def solution(mesh):
    in_specs = (
        P(("grp", "mr"), "mc"),
        P(("grp", "mr"), "mc"),
        P(("grp", "mr"), "mc"),
        P(("grp", "mr"), None, "mc"),
        P(("grp", "mr"), None, "mc"),
        P(("grp", "mr")),
        P(("grp", "mr")),
        P(("grp", "mr"), "mc"),
        P(("grp", "mr"), "mc"),
        P("mc", ("grp", "mr")),
        P("mc", ("grp", "mr")),
    )
    out_specs = (P(("grp", "mr"), "mc"), P("mc", ("grp", "mr")))
    return jax.shard_map(body, mesh=mesh, in_specs=in_specs, out_specs=out_specs, check_vma=False)
```

profile of v0, /device:TPU:0, one launch (start us, length us, event | category | flops | bytes accessed | tf_op | source)
XLA Modules:
  0.0 235.8 jit_solution(16639397591601032340)
XLA Ops:
  7.2 0.0 copy-start
  7.2 0.7 compare_and_fusion
  7.9 0.1 select_reduce_fusion
  8.0 1.4 gather_fusion
  9.4 1.4 gather_fusion.2
  10.7 1.4 gather_fusion.3
  12.1 0.1 select_convert_fusion
  12.2 0.7 gather_fusion.1
  12.9 0.1 select_bitcast_fusion
  13.0 0.1 iota_compare_fusion
  13.1 0.2 fusion.30
  13.3 6.5 %fusion.29 = (f32[24,4,8]{2,1,0:T(4,128)S(1)}, f32[24,4,8,512]{3,2,1,0:T(8,128)S(1)}) fusion(bf16[24,4,8,128]{3,2,1,0:T(8,128)(2,1)S(1)} %bitcast.56, pred[24,512]{1,0:T(8,128)(4,1)S(1)} %iota_compare_fusion, bf16[24,512,512]{2,1,0:T(8,128)(2,1)} %param.18), kind=kOutput, calls=%fused_computation.62 | convolution fusion | flops 101842176 | bytes 14367744 | tf_op jit(solution)/shard_map/bkgd,bckd->bkgc/dot_general | solution.py:24
  19.8 0.5 fusion.8
  20.4 5.8 %fusion.12 = bf16[24,4,8,128]{3,2,1,0:T(8,128)(2,1)S(1)} fusion(f32[24,4,8,512]{3,2,1,0:T(8,128)S(1)} %get-tuple-element.16, f32[24,4,8]{2,1,0:T(4,128)S(1)} %get-tuple-element.11, f32[24,4,8]{2,1,0:T(4,128)S(1)} %multiply_maximum_fusion, f32[24,4,128]{2,1,0:T(4,128)S(1)} %reshape.91, f32[24,4,8]{2,1,0:T(4,128)S(1)} %get-tuple-element.10, ...), kind=kOutput, calls=%fused_computation.25 | convolution fusion | flops 102137856 | bytes 14410752 | tf_op jit(solution)/shard_map/bkgc,bckd->bkgd/dot_general | solution.py:44
  26.2 0.1 copy.47
  26.3 0.7 gather_fusion.4
  27.0 0.1 broadcast_select_fusion.2
  27.1 8.5 %all_gather.6 = bf16[24,8192]{1,0:T(8,128)(2,1)S(1)} all-gather(bf16[24,4096]{1,0:T(8,128)(2,1)S(1)} %broadcast_select_fusion.2), channel_id=1, replica_groups=mesh['grp'=2,'mr'=8,'mc'=2] {'mc'}, dimensions={1}, use_global_device_ids=true | all-gather | bytes 589824 | tf_op jit(solution)/shard_map/all_gather | solution.py:79
  35.6 0.8 copy.46
  36.4 6.2 %all-to-all-start = ((bf16[24,16,512]{2,0,1:T(8,128)(2,1)}), bf16[24,16,512]{2,0,1:T(8,128)(2,1)S(1)}, u32[]{:S(2)}, u32[]{:S(2)}) async-start(bf16[24,16,512]{2,0,1:T(8,128)(2,1)} %bitcast.49), calls=%async_computation | async-start | bytes 786432 | tf_op jit(solution)/shard_map/all_to_all | solution.py:80
  42.5 0.0 reduce-scatter.2.cloned.1.call-start
  42.6 13.0 %all-to-all-done = bf16[24,16,512]{2,0,1:T(8,128)(2,1)S(1)} async-done(((bf16[24,16,512]{2,0,1:T(8,128)(2,1)}), bf16[24,16,512]{2,0,1:T(8,128)(2,1)S(1)}, u32[]{:S(2)}, u32[]{:S(2)}) %all-to-all-start) | async-done | bytes 393248 | tf_op jit(solution)/shard_map/all_to_all | solution.py:80
  55.6 4.4 %convolution_convert_fusion = bf16[192,4096]{1,0:T(8,128)(2,1)} fusion(bf16[512,4096]{1,0:T(8,128)(2,1)} %param.23, bf16[384,512]{1,0:T(8,128)(2,1)S(1)} %bitcast.52, s32[]{:T(128)S(6)} %select_n.80), kind=kOutput, calls=%fused_computation.12 | convolution fusion | flops 806092800 | bytes 5963780 | tf_op jit(solution)/shard_map/dot_general | solution.py:89
  60.0 3.6 %collective-permute-done = bf16[192,4096]{1,0:T(8,128)(2,1)S(1)} collective-permute-done((bf16[192,4096]{1,0:T(8,128)(2,1)}, bf16[192,4096]{1,0:T(8,128)(2,1)S(1)}, u32[]{:S(2)}, u32[]{:S(2)}) %collective-permute-start) | collective-permute-done | bytes 1572896 | tf_op jit(solution)/shard_map/ppermute | solution.py:92
  63.6 4.4 %add_convert_fusion = bf16[192,4096]{1,0:T(8,128)(2,1)} fusion(bf16[192,4096]{1,0:T(8,128)(2,1)S(1)} %collective-permute-done, bf16[512,4096]{1,0:T(8,128)(2,1)} %param.23, bf16[384,512]{1,0:T(8,128)(2,1)S(1)} %bitcast.53, s32[]{:T(128)S(6)} %select_n.81), kind=kOutput, calls=%fused_computation.14 | convolution fusion | flops 807665664 | bytes 7536644 | tf_op jit(solution)/shard_map/dot_general | solution.py:89
  67.9 0.0 reduce-scatter.2.cloned.1.call-update
  68.0 0.2 all-gather.2.cloned.1.call-start
  68.2 63.5 %reduce-scatter.2.cloned.1.call-done = bf16[24,4096]{1,0:T(8,128)(2,1)} async-done(((bf16[192,4096]{1,0:T(8,128)(2,1)}), bf16[24,4096]{1,0:T(8,128)(2,1)}) %reduce-scatter.2.cloned.1.call-update) | async-done | bytes 196624 | tf_op jit(solution)/shard_map/reduce_scatter | solution.py:94
  131.7 1.6 add_convert_fusion.1
  133.3 0.0 all-gather.2.cloned.1.call-update
  133.4 44.1 %all-gather.2.cloned.1.call-done = bf16[192,4096]{1,0:T(8,128)(2,1)} async-done(((bf16[24,4096]{1,0:T(8,128)(2,1)}), bf16[192,4096]{1,0:T(8,128)(2,1)}) %all-gather.2.cloned.1.call-update) | async-done | bytes 1572880 | tf_op jit(solution)/shard_map/all_gather | solution.py:98
  177.5 3.6 %collective-permute-done.1 = bf16[192,4096]{1,0:T(8,128)(2,1)S(1)} collective-permute-done((bf16[192,4096]{1,0:T(8,128)(2,1)}, bf16[192,4096]{1,0:T(8,128)(2,1)S(1)}, u32[]{:S(2)}, u32[]{:S(2)}) %collective-permute-start.1) | collective-permute-done | bytes 1572896 | tf_op jit(solution)/shard_map/ppermute | solution.py:101
  181.1 1.8 broadcast_select_fusion.1
  182.9 0.0 slice-start.1
  182.9 9.3 %fusion.28 = f32[384,1792]{1,0:T(8,128)S(1)} fusion(bf16[4096,1792]{1,0:T(8,128)(2,1)} %param.24, bf16[192,4096]{1,0:T(8,128)(2,1)S(1)} %get-tuple-element.9, bf16[192,4096]{1,0:T(8,128)(2,1)S(1)} %get-tuple-element.8), kind=kOutput, calls=%fused_computation.61 | convolution fusion | flops 5643436032 | bytes 20578304 | tf_op jit(solution)/shard_map/dot_general | solution.py:108
  192.2 0.9 dynamic-slice_convert_fusion.1
  193.2 1.5 collective-permute-start.2
  194.7 5.9 %fusion.27 = f32[384,1792]{1,0:T(8,128)S(1)} fusion(bf16[4096,1792]{1,0:T(8,128)(2,1)S(1)} %bitcast.61, bf16[192,4096]{1,0:T(8,128)(2,1)S(1)} %get-tuple-element.9, bf16[192,4096]{1,0:T(8,128)(2,1)S(1)} %get-tuple-element.8), kind=kOutput, calls=%fused_computation.60 | convolution fusion | flops 5643436032 | bytes 20578304 | tf_op jit(solution)/shard_map/dot_general | solution.py:110
  200.5 1.0 dynamic-slice_convert_fusion
  201.5 0.6 collective-permute-start.4
  202.1 0.2 pad_maximum_fusion
  202.3 0.0 copy-start.1
  202.3 0.7 multiply_reduce_fusion
  203.0 0.1 dynamic_slice.29
  203.1 1.5 collective-permute-start.3
  204.6 21.1 %collective-permute-done.3 = f32[192]{0:T(256)S(1)} collective-permute-done((f32[192]{0:T(256)S(1)}, f32[192]{0:T(256)S(1)}, u32[]{:S(2)}, u32[]{:S(2)}) %collective-permute-start.3) | collective-permute-done | bytes 800 | tf_op jit(solution)/shard_map/ppermute | solution.py:128
  225.7 0.1 add_rsqrt_fusion
  225.8 3.2 %multiply_convert_fusion = bf16[192,1792]{1,0:T(8,128)(2,1)} fusion(bf16[192,1792]{1,0:T(8,128)(2,1)} %collective-permute-done.4, f32[384,1792]{1,0:T(8,128)} %copy-done.2, s32[]{:T(128)S(6)} %select_n.85, bf16[192,1792]{1,0:T(8,128)(2,1)} %collective-permute-done.2, f32[384,1792]{1,0:T(8,128)S(1)} %fusion.28, f32[192]{0:T(256)S(1)} %add_rsqrt_fusion), kind=kLoop, calls=%fused_computation.21 | loop fusion | flops 4128768 | bytes 4817668 | tf_op jit(solution)/shard_map/convert_element_type | solution.py:115
  (28 shorter events, 0.2 us)
Async XLA Ops:
  7.2 5.0 %copy-start = (bf16[24,4096]{1,0:T(8,128)(2,1)S(1)}, bf16[24,4096]{1,0:T(8,128)(2,1)}, u32[]{:S(2)}) copy-start(bf16[24,4096]{1,0:T(8,128)(2,1)} %param.15) | copy-start | bytes 589828
  36.4 19.3 %all-to-all-start = ((bf16[24,16,512]{2,0,1:T(8,128)(2,1)}), bf16[24,16,512]{2,0,1:T(8,128)(2,1)S(1)}, u32[]{:S(2)}, u32[]{:S(2)}) async-start(bf16[24,16,512]{2,0,1:T(8,128)(2,1)} %bitcast.49), calls=%async_computation | async-start | bytes 786432 | tf_op jit(solution)/shard_map/all_to_all | solution.py:80
  42.5 89.1 %reduce-scatter.2.cloned.1.call-start = ((), (), s32[]{:S(2)}) async-start(), calls=%async_computation.2 | async-start | bytes 1769472 | tf_op jit(solution)/shard_map/reduce_scatter | solution.py:94
  60.0 3.6 %collective-permute-start = (bf16[192,4096]{1,0:T(8,128)(2,1)}, bf16[192,4096]{1,0:T(8,128)(2,1)S(1)}, u32[]{:S(2)}, u32[]{:S(2)}) collective-permute-start(bf16[192,4096]{1,0:T(8,128)(2,1)} %convolution_convert_fusion), channel_id=1, source_target_pairs={{0,16},{16,0},{1,17},{17,1},{2,18},{18,2},{3,19},{19,3},{4,20},{20... | collective-permute-start | bytes 4718600 | tf_op jit(solution)/shard_map/ppermute | solution.py:92
  60.0 71.7 %copy-start.3 = (bf16[24,4096]{1,0:T(8,128)(2,1)S(1)}, bf16[24,4096]{1,0:T(8,128)(2,1)}, u32[]{:S(2)}) copy-start(bf16[24,4096]{1,0:T(8,128)(2,1)} %param.22) | copy-start | bytes 589828
  68.0 109.5 %all-gather.2.cloned.1.call-start = ((), (), s32[]{:S(2)}) async-start(), calls=%async_computation.3 | async-start | bytes 1769472 | tf_op jit(solution)/shard_map/all_gather | solution.py:98
  177.5 3.6 %collective-permute-start.1 = (bf16[192,4096]{1,0:T(8,128)(2,1)}, bf16[192,4096]{1,0:T(8,128)(2,1)S(1)}, u32[]{:S(2)}, u32[]{:S(2)}) collective-permute-start(bf16[192,4096]{1,0:T(8,128)(2,1)} %all-gather.2.cloned.1.call-done), channel_id=1, source_target_pairs={{0,16},{16,0},{1,17},{17,1},{2,18},{18,2},{3,19},{19,3},{4,20},{20... | collective-permute-start | bytes 4718600 | tf_op jit(solution)/shard_map/ppermute | solution.py:101
  181.1 13.5 %slice-start = ((s8[14680064]{0:T(1024)(128)(4,1)}), s8[4194304]{0:T(1024)(128)(4,1)S(1)}, s32[]{:S(2)}) async-start(s8[14680064]{0:T(1024)(128)(4,1)} %bitcast.60), calls=%async_computation.4 | async-start | bytes 8388608
  182.9 11.7 %slice-start.1 = ((s8[14680064]{0:T(1024)(128)(4,1)}), s8[4194304]{0:T(1024)(128)(4,1)S(1)}, s32[]{:S(2)}) async-start(s8[14680064]{0:T(1024)(128)(4,1)} %bitcast.60), calls=%async_computation.5 | async-start | bytes 8388608
  182.9 11.7 %slice-start.2 = ((s8[14680064]{0:T(1024)(128)(4,1)}), s8[4194304]{0:T(1024)(128)(4,1)S(1)}, s32[]{:S(2)}) async-start(s8[14680064]{0:T(1024)(128)(4,1)} %bitcast.60), calls=%async_computation.6 | async-start | bytes 8388608
  182.9 11.7 %slice-start.3 = ((s8[14680064]{0:T(1024)(128)(4,1)}), s8[2097152]{0:T(1024)(128)(4,1)S(1)}, s32[]{:S(2)}) async-start(s8[14680064]{0:T(1024)(128)(4,1)} %bitcast.60), calls=%async_computation.7 | async-start | bytes 4194304
  193.2 32.6 %collective-permute-start.2 = (bf16[192,1792]{1,0:T(8,128)(2,1)}, bf16[192,1792]{1,0:T(8,128)(2,1)}, u32[]{:S(2)}, u32[]{:S(2)}) collective-permute-start(bf16[192,1792]{1,0:T(8,128)(2,1)} %dynamic-slice_convert_fusion.1), channel_id=1, source_target_pairs={{0,1},{1,0},{2,3},{3,2},{4,5},{5,4},{6,7},{7,6},{8,9},{9,8},{10,11... | collective-permute-start | bytes 2064392 | tf_op jit(solution)/shard_map/ppermute | solution.py:128
  200.5 1.8 copy-start.2
  201.5 24.3 %collective-permute-start.4 = (bf16[192,1792]{1,0:T(8,128)(2,1)}, bf16[192,1792]{1,0:T(8,128)(2,1)}, u32[]{:S(2)}, u32[]{:S(2)}) collective-permute-start(bf16[192,1792]{1,0:T(8,128)(2,1)} %dynamic-slice_convert_fusion), channel_id=1, source_target_pairs={{0,1},{1,0},{2,3},{3,2},{4,5},{5,4},{6,7},{7,6},{8,9},{9,8},{10,11... | collective-permute-start | bytes 2064392 | tf_op jit(solution)/shard_map/ppermute | solution.py:128
  202.3 26.7 %copy-start.1 = (bf16[24,4096]{1,0:T(8,128)(2,1)S(1)}, bf16[24,4096]{1,0:T(8,128)(2,1)}, u32[]{:S(2)}) copy-start(bf16[24,4096]{1,0:T(8,128)(2,1)} %param.15) | copy-start | bytes 589828
  203.1 22.6 %collective-permute-start.3 = (f32[192]{0:T(256)S(1)}, f32[192]{0:T(256)S(1)}, u32[]{:S(2)}, u32[]{:S(2)}) collective-permute-start(f32[192]{0:T(256)S(1)} %dynamic_slice.29), channel_id=1, source_target_pairs={{0,1},{1,0},{2,3},{3,2},{4,5},{5,4},{6,7},{7,6},{8,9},{9,8},{10,11... | collective-permute-start | bytes 2312 | tf_op jit(solution)/shard_map/ppermute | solution.py:128
Sparse Core Ops, SparseCore 0:
  68.1 63.5 reduce-scatter.1
  134.5 43.0 all-gather.1
where the time goes:
time: 236 us
  waiting for transfers between devices  149 us (63%)
  matrix products  36.3 us (15%)
  between operations  14.3 us (6%)
  starting transfers between devices  9.95 us (4%)
  other arithmetic  9.32 us (4%)
  blocking collectives  8.53 us (4%)
  local copies, waits for them, and re-layouts  8.38 us (4%)
    reduce_scatter x1, waiting for transfers between devices, body(): lax.psum_scatter(own_share.astype(jnp.bfloat16), 'mr', scatter_dimension=...  63.5 us
    all_gather x1, waiting for transfers between devices, body(): group_part = lax.all_gather(residual_out, 'mr', axis=0, tiled=True)  44.1 us
    ppermute x3, waiting for transfers between devices, scatter_sum(): total = total + lax.ppermute(sent, 'mc', pairs).astype(jnp.float32)  21.1 us
    all_to_all x1, waiting for transfers between devices, body(): lax.all_to_all(gathered, ('grp', 'mr'), split_axis=1, concat_axis=0, tile...  13 us
    dot_general x1, matrix products, body(): jnp.dot(everyone, gate_weight, preferred_element_type=jnp.float32)  9.31 us
    dot_general x2, matrix products, body(): term = jnp.dot(block, out_weight, preferred_element_type=jnp.float32)  8.72 us
    all_gather x1, blocking collectives, body(): gathered = lax.all_gather(attended, 'mc', axis=1, tiled=True)  8.53 us
    dot_general x1, matrix products, attend_rows(): jnp.einsum('bkgd,bckd->bkgc', query_grouped_four, key_four, preferred_ele...  6.45 us
  transfers between devices with their start and end apart: 8, of which 6 were waited for; matrix products, arithmetic and copies ran while one was open for 3% of the time, Pallas kernels for 0%

commit v1 on v0

--- a/solution.py
+++ b/solution.py
@@ -95,7 +95,8 @@
         own_share.astype(jnp.bfloat16), "mr", scatter_dimension=0, tiled=True
     ).astype(jnp.float32)
     residual_out = (residual_in.astype(jnp.float32) + shares).astype(jnp.bfloat16)
-    group_part = lax.all_gather(residual_out, "mr", axis=0, tiled=True)
+    outgoing = jnp.stack([residual_out] * lax.axis_size("mr"))
+    group_part = jnp.concatenate(lax.all_to_all(outgoing, "mr", 0, 0), axis=0)
     everyone = lax.all_gather(group_part, "grp", axis=0, tiled=True) if groups != 2 else None
     if groups == 2:
         other_part = lax.ppermute(group_part, "grp", [(0, 1), (1, 0)])

time: 236 us -> 229 us (0.970)
  waiting for transfers between devices: 149 us -> 105 us
  blocking collectives: 8.53 us -> 47.4 us
    all_gather x1 -> x0, waiting for transfers between devices: 44.1 us -> none  [body(): group_part = lax.all_gather(residual_out, 'mr', axis=0, tiled=True)]
    all_to_all x0 -> x1, blocking collectives: none -> 38.9 us  [body(): group_part = jnp.concatenate(lax.all_to_all(outgoing, 'mr', 0, 0), axis=0)]
  transfers between devices with their start and end apart: 8 -> 7, of which waited for: 6 -> 5; matrix products, arithmetic and copies ran while one was open for 3% -> 3% of each run, Pallas kernels for 0% -> 0%
where the time goes in v1:
time: 229 us
  waiting for transfers between devices  105 us (46%)
  blocking collectives  47.4 us (21%)
  matrix products  36.3 us (16%)
  between operations  14.3 us (6%)
  starting transfers between devices  9.75 us (4%)
  local copies, waits for them, and re-layouts  8.53 us (4%)
  other arithmetic  7.18 us (3%)
    reduce_scatter x1, waiting for transfers between devices, body(): lax.psum_scatter(own_share.astype(jnp.bfloat16), 'mr', scatter_dimension=...  63.8 us
    all_to_all x1, blocking collectives, body(): group_part = jnp.concatenate(lax.all_to_all(outgoing, 'mr', 0, 0), axis=0)  38.9 us
    ppermute x3, waiting for transfers between devices, scatter_sum(): total = total + lax.ppermute(sent, 'mc', pairs).astype(jnp.float32)  21.1 us
    all_to_all x1, waiting for transfers between devices, body(): lax.all_to_all(gathered, ('grp', 'mr'), split_axis=1, concat_axis=0, tile...  13 us
    dot_general x1, matrix products, body(): jnp.dot(everyone, gate_weight, preferred_element_type=jnp.float32)  9.34 us
    dot_general x2, matrix products, body(): term = jnp.dot(block, out_weight, preferred_element_type=jnp.float32)  8.7 us
    all_gather x1, blocking collectives, body(): gathered = lax.all_gather(attended, 'mc', axis=1, tiled=True)  8.53 us
    dot_general x1, matrix products, attend_rows(): jnp.einsum('bkgd,bckd->bkgc', query_grouped_four, key_four, preferred_ele...  6.45 us
  transfers between devices with their start and end apart: 7, of which 5 were waited for; matrix products, arithmetic and copies ran while one was open for 3% of the time, Pallas kernels for 0%

profile of v1, /device:TPU:0, one launch (start us, length us, event | category | flops | bytes accessed | tf_op | source)
XLA Modules:
  0.0 228.5 jit_solution(16923854433786790951)
XLA Ops:
  7.2 0.0 copy-start
  7.2 0.7 compare_and_fusion
  7.9 0.1 select_reduce_fusion
  8.0 1.4 gather_fusion
  9.4 1.4 gather_fusion.2
  10.7 1.4 gather_fusion.3
  12.1 0.1 select_convert_fusion
  12.2 0.7 gather_fusion.1
  12.9 0.1 select_bitcast_fusion
  13.0 0.1 iota_compare_fusion
  13.1 0.2 fusion.30
  13.3 6.5 %fusion.29 = (f32[24,4,8]{2,1,0:T(4,128)S(1)}, f32[24,4,8,512]{3,2,1,0:T(8,128)S(1)}) fusion(bf16[24,4,8,128]{3,2,1,0:T(8,128)(2,1)S(1)} %bitcast.60, pred[24,512]{1,0:T(8,128)(4,1)S(1)} %iota_compare_fusion, bf16[24,512,512]{2,1,0:T(8,128)(2,1)} %param.18), kind=kOutput, calls=%fused_computation.62 | convolution fusion | flops 101842176 | bytes 14367744 | tf_op jit(solution)/shard_map/bkgd,bckd->bkgc/dot_general | solution.py:24
  19.8 0.5 fusion.8
  20.4 5.8 %fusion.12 = bf16[24,4,8,128]{3,2,1,0:T(8,128)(2,1)S(1)} fusion(f32[24,4,8,512]{3,2,1,0:T(8,128)S(1)} %get-tuple-element.16, f32[24,4,8]{2,1,0:T(4,128)S(1)} %get-tuple-element.11, f32[24,4,8]{2,1,0:T(4,128)S(1)} %multiply_maximum_fusion, f32[24,4,128]{2,1,0:T(4,128)S(1)} %reshape.97, f32[24,4,8]{2,1,0:T(4,128)S(1)} %get-tuple-element.10, ...), kind=kOutput, calls=%fused_computation.25 | convolution fusion | flops 102137856 | bytes 14410752 | tf_op jit(solution)/shard_map/bkgc,bckd->bkgd/dot_general | solution.py:44
  26.2 0.1 copy.47
  26.3 0.7 gather_fusion.4
  27.0 0.1 broadcast_select_fusion.2
  27.1 8.5 %all_gather.3 = bf16[24,8192]{1,0:T(8,128)(2,1)S(1)} all-gather(bf16[24,4096]{1,0:T(8,128)(2,1)S(1)} %broadcast_select_fusion.2), channel_id=1, replica_groups=mesh['grp'=2,'mr'=8,'mc'=2] {'mc'}, dimensions={1}, use_global_device_ids=true | all-gather | bytes 589824 | tf_op jit(solution)/shard_map/all_gather | solution.py:79
  35.6 0.8 copy.46
  36.4 6.2 %all-to-all-start = ((bf16[24,16,512]{2,0,1:T(8,128)(2,1)}), bf16[24,16,512]{2,0,1:T(8,128)(2,1)S(1)}, u32[]{:S(2)}, u32[]{:S(2)}) async-start(bf16[24,16,512]{2,0,1:T(8,128)(2,1)} %bitcast.52), calls=%async_computation | async-start | bytes 786432 | tf_op jit(solution)/shard_map/all_to_all | solution.py:80
  42.6 0.0 reduce-scatter.2.cloned.1.call-start
  42.6 13.0 %all-to-all-done = bf16[24,16,512]{2,0,1:T(8,128)(2,1)S(1)} async-done(((bf16[24,16,512]{2,0,1:T(8,128)(2,1)}), bf16[24,16,512]{2,0,1:T(8,128)(2,1)S(1)}, u32[]{:S(2)}, u32[]{:S(2)}) %all-to-all-start) | async-done | bytes 393248 | tf_op jit(solution)/shard_map/all_to_all | solution.py:80
  55.6 4.3 %convolution_convert_fusion = bf16[192,4096]{1,0:T(8,128)(2,1)} fusion(bf16[512,4096]{1,0:T(8,128)(2,1)} %param.23, bf16[384,512]{1,0:T(8,128)(2,1)S(1)} %bitcast.56, s32[]{:T(128)S(6)} %select_n.80), kind=kOutput, calls=%fused_computation.12 | convolution fusion | flops 806092800 | bytes 5963780 | tf_op jit(solution)/shard_map/dot_general | solution.py:89
  60.0 3.6 %collective-permute-done = bf16[192,4096]{1,0:T(8,128)(2,1)S(1)} collective-permute-done((bf16[192,4096]{1,0:T(8,128)(2,1)}, bf16[192,4096]{1,0:T(8,128)(2,1)S(1)}, u32[]{:S(2)}, u32[]{:S(2)}) %collective-permute-start) | collective-permute-done | bytes 1572896 | tf_op jit(solution)/shard_map/ppermute | solution.py:92
  63.6 4.4 %add_convert_fusion = bf16[192,4096]{1,0:T(8,128)(2,1)} fusion(bf16[192,4096]{1,0:T(8,128)(2,1)S(1)} %collective-permute-done, bf16[512,4096]{1,0:T(8,128)(2,1)} %param.23, bf16[384,512]{1,0:T(8,128)(2,1)S(1)} %bitcast.57, s32[]{:T(128)S(6)} %select_n.81), kind=kOutput, calls=%fused_computation.14 | convolution fusion | flops 807665664 | bytes 7536644 | tf_op jit(solution)/shard_map/dot_general | solution.py:89
  67.9 0.0 reduce-scatter.2.cloned.1.call-update
  68.0 63.8 %reduce-scatter.2.cloned.1.call-done = bf16[24,4096]{1,0:T(8,128)(2,1)} async-done(((bf16[192,4096]{1,0:T(8,128)(2,1)}), bf16[24,4096]{1,0:T(8,128)(2,1)}) %reduce-scatter.2.cloned.1.call-update) | async-done | bytes 196624 | tf_op jit(solution)/shard_map/reduce_scatter | solution.py:94
  131.7 1.0 add_convert_fusion.1
  132.7 0.0 copy-start.3
  132.7 0.2 stack.2
  132.9 38.9 %all_to_all.24 = bf16[8,24,4096]{2,1,0:T(8,128)(2,1)S(1)} all-to-all(bf16[8,24,4096]{2,1,0:T(8,128)(2,1)S(1)} %stack.2), channel_id=1, replica_groups=mesh['grp'=2,'mr'=8,'mc'=2] {'mr'}, dimensions={0} | all-to-all | bytes 3145728 | tf_op jit(solution)/shard_map/all_to_all | solution.py:99
  171.8 3.4 %collective-permute-done.1 = bf16[192,4096]{1,0:T(8,128)(2,1)S(1)} collective-permute-done((bf16[192,4096]{1,0:T(8,128)(2,1)S(1)}, bf16[192,4096]{1,0:T(8,128)(2,1)S(1)}, u32[]{:S(2)}, u32[]{:S(2)}) %collective-permute-start.1) | collective-permute-done | bytes 1572896 | tf_op jit(solution)/shard_map/ppermute | solution.py:102
  175.2 0.3 broadcast_select_fusion.1
  175.5 0.0 slice-start.1
  175.6 9.3 %fusion.28 = f32[384,1792]{1,0:T(8,128)S(1)} fusion(bf16[4096,1792]{1,0:T(8,128)(2,1)} %param.24, bf16[192,4096]{1,0:T(8,128)(2,1)S(1)} %get-tuple-element.9, bf16[192,4096]{1,0:T(8,128)(2,1)S(1)} %get-tuple-element.8), kind=kOutput, calls=%fused_computation.61 | convolution fusion | flops 5643436032 | bytes 20578304 | tf_op jit(solution)/shard_map/dot_general | solution.py:109
  184.9 0.9 dynamic-slice_convert_fusion.1
  185.9 1.5 collective-permute-start.2
  187.4 5.9 %fusion.27 = f32[384,1792]{1,0:T(8,128)S(1)} fusion(bf16[4096,1792]{1,0:T(8,128)(2,1)S(1)} %bitcast.65, bf16[192,4096]{1,0:T(8,128)(2,1)S(1)} %get-tuple-element.9, bf16[192,4096]{1,0:T(8,128)(2,1)S(1)} %get-tuple-element.8), kind=kOutput, calls=%fused_computation.60 | convolution fusion | flops 5643436032 | bytes 20578304 | tf_op jit(solution)/shard_map/dot_general | solution.py:111
  193.2 1.0 dynamic-slice_convert_fusion
  194.2 0.5 collective-permute-start.4
  194.8 0.2 pad_maximum_fusion
  195.0 0.0 copy-start.1
  195.0 0.7 multiply_reduce_fusion
  195.7 0.1 dynamic_slice.29
  195.8 1.5 collective-permute-start.3
  197.3 21.1 %collective-permute-done.3 = f32[192]{0:T(256)S(1)} collective-permute-done((f32[192]{0:T(256)S(1)}, f32[192]{0:T(256)S(1)}, u32[]{:S(2)}, u32[]{:S(2)}) %collective-permute-start.3) | collective-permute-done | bytes 800 | tf_op jit(solution)/shard_map/ppermute | solution.py:129
  218.4 0.1 add_rsqrt_fusion
  218.5 3.2 %multiply_convert_fusion = bf16[192,1792]{1,0:T(8,128)(2,1)} fusion(bf16[192,1792]{1,0:T(8,128)(2,1)} %collective-permute-done.4, f32[384,1792]{1,0:T(8,128)} %copy-done.2, s32[]{:T(128)S(6)} %select_n.85, bf16[192,1792]{1,0:T(8,128)(2,1)} %collective-permute-done.2, f32[384,1792]{1,0:T(8,128)S(1)} %fusion.28, f32[192]{0:T(256)S(1)} %add_rsqrt_fusion), kind=kLoop, calls=%fused_computation.21 | loop fusion | flops 4128768 | bytes 4817668 | tf_op jit(solution)/shard_map/convert_element_type | solution.py:116
  (29 shorter events, 0.2 us)
Async XLA Ops:
  7.2 5.0 %copy-start = (bf16[24,4096]{1,0:T(8,128)(2,1)S(1)}, bf16[24,4096]{1,0:T(8,128)(2,1)}, u32[]{:S(2)}) copy-start(bf16[24,4096]{1,0:T(8,128)(2,1)} %param.15) | copy-start | bytes 589828
  36.4 19.3 %all-to-all-start = ((bf16[24,16,512]{2,0,1:T(8,128)(2,1)}), bf16[24,16,512]{2,0,1:T(8,128)(2,1)S(1)}, u32[]{:S(2)}, u32[]{:S(2)}) async-start(bf16[24,16,512]{2,0,1:T(8,128)(2,1)} %bitcast.52), calls=%async_computation | async-start | bytes 786432 | tf_op jit(solution)/shard_map/all_to_all | solution.py:80
  42.6 89.2 %reduce-scatter.2.cloned.1.call-start = ((), (), s32[]{:S(2)}) async-start(), calls=%async_computation.3 | async-start | bytes 1769472 | tf_op jit(solution)/shard_map/reduce_scatter | solution.py:94
  60.0 3.6 %collective-permute-start = (bf16[192,4096]{1,0:T(8,128)(2,1)}, bf16[192,4096]{1,0:T(8,128)(2,1)S(1)}, u32[]{:S(2)}, u32[]{:S(2)}) collective-permute-start(bf16[192,4096]{1,0:T(8,128)(2,1)} %convolution_convert_fusion), channel_id=1, source_target_pairs={{0,16},{16,0},{1,17},{17,1},{2,18},{18,2},{3,19},{19,3},{4,20},{20... | collective-permute-start | bytes 4718600 | tf_op jit(solution)/shard_map/ppermute | solution.py:92
  60.0 71.8 %copy-start.4 = (bf16[24,4096]{1,0:T(8,128)(2,1)S(1)}, bf16[24,4096]{1,0:T(8,128)(2,1)}, u32[]{:S(2)}) copy-start(bf16[24,4096]{1,0:T(8,128)(2,1)} %param.22) | copy-start | bytes 589828
  132.7 42.8 %copy-start.3 = (bf16[24,4096]{1,0:T(8,128)(2,1)}, bf16[24,4096]{1,0:T(8,128)(2,1)S(1)}, u32[]{:S(2)}) copy-start(bf16[24,4096]{1,0:T(8,128)(2,1)S(1)} %add_convert_fusion.1) | copy-start | bytes 589828
  171.8 3.4 %collective-permute-start.1 = (bf16[192,4096]{1,0:T(8,128)(2,1)S(1)}, bf16[192,4096]{1,0:T(8,128)(2,1)S(1)}, u32[]{:S(2)}, u32[]{:S(2)}) collective-permute-start(bf16[192,4096]{1,0:T(8,128)(2,1)S(1)} %bitcast.55), channel_id=1, source_target_pairs={{0,16},{16,0},{1,17},{17,1},{2,18},{18,2},{3,19},{19,3},{4,20},{20... | collective-permute-start | bytes 4718600 | tf_op jit(solution)/shard_map/ppermute | solution.py:102
  175.2 12.1 %slice-start = ((s8[14680064]{0:T(1024)(128)(4,1)}), s8[4194304]{0:T(1024)(128)(4,1)S(1)}, s32[]{:S(2)}) async-start(s8[14680064]{0:T(1024)(128)(4,1)} %bitcast.64), calls=%async_computation.4 | async-start | bytes 8388608
  175.5 11.8 %slice-start.1 = ((s8[14680064]{0:T(1024)(128)(4,1)}), s8[4194304]{0:T(1024)(128)(4,1)S(1)}, s32[]{:S(2)}) async-start(s8[14680064]{0:T(1024)(128)(4,1)} %bitcast.64), calls=%async_computation.5 | async-start | bytes 8388608
  175.6 11.8 %slice-start.2 = ((s8[14680064]{0:T(1024)(128)(4,1)}), s8[4194304]{0:T(1024)(128)(4,1)S(1)}, s32[]{:S(2)}) async-start(s8[14680064]{0:T(1024)(128)(4,1)} %bitcast.64), calls=%async_computation.6 | async-start | bytes 8388608
  175.6 11.8 %slice-start.3 = ((s8[14680064]{0:T(1024)(128)(4,1)}), s8[2097152]{0:T(1024)(128)(4,1)S(1)}, s32[]{:S(2)}) async-start(s8[14680064]{0:T(1024)(128)(4,1)} %bitcast.64), calls=%async_computation.7 | async-start | bytes 4194304
  185.9 32.6 %collective-permute-start.2 = (bf16[192,1792]{1,0:T(8,128)(2,1)}, bf16[192,1792]{1,0:T(8,128)(2,1)}, u32[]{:S(2)}, u32[]{:S(2)}) collective-permute-start(bf16[192,1792]{1,0:T(8,128)(2,1)} %dynamic-slice_convert_fusion.1), channel_id=1, source_target_pairs={{0,1},{1,0},{2,3},{3,2},{4,5},{5,4},{6,7},{7,6},{8,9},{9,8},{10,11... | collective-permute-start | bytes 2064392 | tf_op jit(solution)/shard_map/ppermute | solution.py:129
  193.2 1.8 copy-start.2
  194.2 24.2 %collective-permute-start.4 = (bf16[192,1792]{1,0:T(8,128)(2,1)}, bf16[192,1792]{1,0:T(8,128)(2,1)}, u32[]{:S(2)}, u32[]{:S(2)}) collective-permute-start(bf16[192,1792]{1,0:T(8,128)(2,1)} %dynamic-slice_convert_fusion), channel_id=1, source_target_pairs={{0,1},{1,0},{2,3},{3,2},{4,5},{5,4},{6,7},{7,6},{8,9},{9,8},{10,11... | collective-permute-start | bytes 2064392 | tf_op jit(solution)/shard_map/ppermute | solution.py:129
  195.0 26.7 %copy-start.1 = (bf16[24,4096]{1,0:T(8,128)(2,1)S(1)}, bf16[24,4096]{1,0:T(8,128)(2,1)}, u32[]{:S(2)}) copy-start(bf16[24,4096]{1,0:T(8,128)(2,1)} %param.15) | copy-start | bytes 589828
  195.8 22.6 %collective-permute-start.3 = (f32[192]{0:T(256)S(1)}, f32[192]{0:T(256)S(1)}, u32[]{:S(2)}, u32[]{:S(2)}) collective-permute-start(f32[192]{0:T(256)S(1)} %dynamic_slice.29), channel_id=1, source_target_pairs={{0,1},{1,0},{2,3},{3,2},{4,5},{5,4},{6,7},{7,6},{8,9},{9,8},{10,11... | collective-permute-start | bytes 2312 | tf_op jit(solution)/shard_map/ppermute | solution.py:129
Sparse Core Ops, SparseCore 0:
  68.1 63.6 reduce-scatter.1
